TPU v7x, 256 devices: a whole 4x4x8 slice. The times are simulated.
256 devices in a mesh: row: 16 (over x, y), col: 16 (over z, core).
Axes of the slice: x: 4, y: 4, z: 8, core: 2. Of those that a mesh axis runs over, the one named last changes fastest.
Arguments:
- start_block: float32 [65536, 128], P(('row', 'col')), may hold values from -6 to 6
- vertex_scale: float32 [65536], P(('row', 'col')), may hold values from 0.015625 to 0.0625
- adj_tiles: bfloat16 [16, 16, 64, 128, 128], P('row', 'col'), may hold values from 0 to 1
- tile_row: int32 [16, 16, 64], P('row', 'col'), may hold values from 0 to 31
- tile_col: int32 [16, 16, 64], P('row', 'col'), may hold values from 0 to 31
- live_count: int32 [16, 16], P('row', 'col'), may hold values from 16 to 64, as said below
- rotation_first: float32 [256, 128], replicated, may hold values from -0.375 to 0.375
- rotation_second: float32 [384, 128], replicated, may hold values from -0.3125 to 0.3125
Outputs:
- final_block: float32 [65536, 128], P(('row', 'col'))
- final_image: float32 [65536, 128], P(('row', 'col'))
Inputs may be any that keep to these rules, and one draw needn't show every extreme that they name: Slots from live_count on are ignored; at least one device has all 64 slots live in every draw.
All inputs are finite; a program needn't handle non-finite values.
Results may differ from a plain program's by a relative error of at most 0.01.
Values may be sent and summed in bfloat16 or wider, within the bound.
A program may use at most 64 MiB of HBM per device.

v0:
```python
import jax
import jax.numpy as jnp
from jax import lax
from jax.sharding import PartitionSpec as P

HIGH = lax.Precision.HIGHEST


def tile_products(tiles_here, cols_here, count_here, flat_panel, span_slots, tile_side, width_k):
    alive_mask = jnp.arange(span_slots, dtype=jnp.int32) < count_here
    pieces = jnp.take(flat_panel, cols_here, axis=0)
    pieces = jnp.where(alive_mask[:, None], pieces, jnp.zeros_like(pieces))
    pieces = pieces.reshape(span_slots, tile_side, width_k)
    tile_out = jnp.einsum("tab,tbk->tak", tiles_here, pieces, preferred_element_type=jnp.float32)
    return tile_out.reshape(span_slots, tile_side * width_k)


def place_rows(rows_slot, tile_out, row_tiles, tile_side, width_k):
    placed = jax.ops.segment_sum(tile_out, rows_slot, num_segments=row_tiles)
    return placed.reshape(row_tiles * tile_side, width_k)


def apply_operator(block, vertex_scale, tiles_here, rows_here, cols_here, count_here):
    tile_side = tiles_here.shape[-1]
    width_k = block.shape[1]
    slot_total = tiles_here.shape[0]
    scaled = (vertex_scale[:, None] * block).astype(jnp.bfloat16)
    gathered = lax.all_gather(scaled, "col", axis=0, tiled=True)
    flat_panel = gathered.reshape(gathered.shape[0] // tile_side, tile_side * width_k)
    row_tiles = lax.axis_size("row") * block.shape[0] // tile_side
    tile_out = tile_products(
        tiles_here, cols_here, count_here, flat_panel, slot_total, tile_side, width_k
    )
    partial_value = place_rows(rows_here, tile_out, row_tiles, tile_side, width_k)
    summed = lax.psum_scatter(
        partial_value.astype(jnp.bfloat16), "row", scatter_dimension=0, tiled=True
    ).astype(jnp.float32)
    return block - vertex_scale[:, None] * summed


def inner(left, right):
    return jnp.einsum("sk,sl->kl", left, right, precision=HIGH)


def residual_block(block, image, verts_all):
    gram = lax.psum(inner(block, image), ("row", "col")) / verts_all
    resid = image - jnp.dot(block, gram, precision=HIGH)
    colsq = lax.psum(jnp.sum(resid * resid, axis=0), ("row", "col"))
    return resid * lax.rsqrt(colsq / verts_all + 1e-06)


def local(
    start_block,
    vertex_scale,
    adj_tiles,
    tile_row,
    tile_col,
    live_count,
    rotation_first,
    rotation_second,
):
    width_k = start_block.shape[1]
    verts_all = start_block.shape[0] * lax.axis_size("row") * lax.axis_size("col")
    tiles_here = adj_tiles[0, 0]
    rows_here = tile_row[0, 0]
    cols_here = tile_col[0, 0]
    count_here = live_count[0, 0]

    def oper(block):
        return apply_operator(block, vertex_scale, tiles_here, rows_here, cols_here, count_here)

    image0 = oper(start_block)
    search0 = residual_block(start_block, image0, verts_all)
    simage0 = oper(search0)
    rot_x, rot_w = (rotation_first[:width_k], rotation_first[width_k:])
    block1 = jnp.dot(start_block, rot_x, precision=HIGH) + jnp.dot(search0, rot_w, precision=HIGH)
    image1 = jnp.dot(image0, rot_x, precision=HIGH) + jnp.dot(simage0, rot_w, precision=HIGH)
    prev1 = jnp.dot(search0, rot_w, precision=HIGH)
    pimage1 = jnp.dot(simage0, rot_w, precision=HIGH)
    search1 = residual_block(block1, image1, verts_all)
    simage1 = oper(search1)
    rot_qx = rotation_second[:width_k]
    rot_qw = rotation_second[width_k : 2 * width_k]
    rot_qp = rotation_second[2 * width_k :]
    final_block = (
        jnp.dot(block1, rot_qx, precision=HIGH)
        + jnp.dot(search1, rot_qw, precision=HIGH)
        + jnp.dot(prev1, rot_qp, precision=HIGH)
    )
    final_image = (
        jnp.dot(image1, rot_qx, precision=HIGH)
        + jnp.dot(simage1, rot_qw, precision=HIGH)
        + jnp.dot(pimage1, rot_qp, precision=HIGH)
    )
    return (final_block, final_image)


def solution(mesh):
    placed = (
        P(("row", "col"), None),
        P(("row", "col")),
        P("row", "col", None, None, None),
        P("row", "col", None),
        P("row", "col", None),
        P("row", "col"),
        P(),
        P(),
    )
    return jax.shard_map(
        local,
        mesh=mesh,
        in_specs=placed,
        out_specs=(P(("row", "col"), None), P(("row", "col"), None)),
        check_vma=False,
    )
```

profile of v0, /device:TPU:2, one launch (start us, length us, event | category | flops | bytes accessed | tf_op | source)
XLA Modules:
  0.0 1100.4 jit_solution(16218495195349804594)
XLA Ops:
  7.2 1.1 copy.23
  8.4 1.3 multiply_convert_fusion.2
  10.4 0.7 compare_select_fusion
  11.1 0.7 compare_and_fusion
  11.7 39.2 %all-gather.4.cloned.1.call-done = bf16[4096,128]{0,1:T(8,128)(2,1)} async-done(((bf16[256,128]{0,1:T(8,128)(2,1)}), bf16[4096,128]{0,1:T(8,128)(2,1)}) %all-gather.4.cloned.1.call-update) | async-done | bytes 1048592 | tf_op jit(solution)/shard_map/all_gather | solution.py:28
  51.0 2.3 copy.19
  53.2 1.5 reshape.49
  54.8 3.2 gather_fusion
  58.0 1.9 fusion.14
  59.9 0.6 copy.40
  60.5 3.6 convolution_bitcast_fusion.2
  64.0 5.6 copy.21
  69.6 10.6 scatter_custom_fusion
  80.3 1.7 convert_element_type.37
  82.0 1.3 convert_element_type.38
  83.3 2.3 copy.22
  85.6 76.8 %reduce-scatter.4.cloned.1.call-done = bf16[256,128]{0,1:T(8,128)(2,1)} async-done(((bf16[4096,128]{0,1:T(8,128)(2,1)}), bf16[256,128]{0,1:T(8,128)(2,1)}) %reduce-scatter.4.cloned.1.call-update) | async-done | bytes 65552 | tf_op jit(solution)/shard_map/reduce_scatter | solution.py:35
  162.4 1.7 convolution_bitcast_fusion.4
  164.3 241.9 %all-reduce.3.cloned.1.call-done = f32[128,128]{0,1:T(8,128)} async-done(((f32[128,128]{0,1:T(8,128)}), f32[128,128]{0,1:T(8,128)}) %all-reduce.3.cloned.1.call-update) | async-done | bytes 65552 | tf_op jit(solution)/shard_map/psum | solution.py:46
  406.2 1.2 multiply_reduce_fusion.1
  407.4 74.2 %psum.29 = f32[128]{0:T(128)S(1)} all-reduce(f32[128]{0:T(128)S(1)} %get-tuple-element.3), channel_id=1, replica_groups=mesh['row'=16,'col'=16] {'row','col'}, use_global_device_ids=true, to_apply=%region_4.6 | all-reduce | flops 128 | bytes 1024 | tf_op jit(solution)/shard_map/psum | solution.py:48
  481.6 0.5 copy-done.12
  482.1 0.7 multiply_convert_fusion.1
  483.1 33.3 %all-gather.6.cloned.1.call-done = bf16[4096,128]{0,1:T(8,128)(2,1)} async-done(((bf16[256,128]{0,1:T(8,128)(2,1)}), bf16[4096,128]{0,1:T(8,128)(2,1)}) %all-gather.6.cloned.1.call-update) | async-done | bytes 1048592 | tf_op jit(solution)/shard_map/all_gather | solution.py:28
  516.4 2.3 copy.24
  518.7 1.5 reshape.52
  520.2 3.2 gather_fusion.1
  523.4 1.9 fusion.13
  525.3 0.6 copy.42
  525.9 3.6 convolution_bitcast_fusion.1
  529.5 5.6 copy.26
  535.1 10.6 scatter_custom_fusion.1
  545.7 1.7 convert_element_type.41
  547.4 1.3 convert_element_type.42
  548.7 2.3 copy.27
  551.3 0.5 fusion.29
  552.1 75.8 %reduce-scatter.6.cloned.1.call-done = bf16[256,128]{0,1:T(8,128)(2,1)} async-done(((bf16[4096,128]{0,1:T(8,128)(2,1)}), bf16[256,128]{0,1:T(8,128)(2,1)}) %reduce-scatter.6.cloned.1.call-update) | async-done | bytes 65552 | tf_op jit(solution)/shard_map/reduce_scatter | solution.py:35
  627.9 1.3 fusion.22
  629.2 0.6 copy-done.6
  629.9 0.3 convolution_add_fusion.4
  630.3 0.9 fusion.55
  631.2 238.6 %all-reduce.5.cloned.1.call-done = f32[128,128]{0,1:T(8,128)} async-done(((f32[128,128]{0,1:T(8,128)}), f32[128,128]{0,1:T(8,128)}) %all-reduce.5.cloned.1.call-update) | async-done | bytes 65552 | tf_op jit(solution)/shard_map/psum | solution.py:46
  869.8 1.2 multiply_reduce_fusion
  871.0 74.2 %psum.31 = f32[128]{0:T(128)S(1)} all-reduce(f32[128]{0:T(128)S(1)} %get-tuple-element.5), channel_id=1, replica_groups=mesh['row'=16,'col'=16] {'row','col'}, use_global_device_ids=true, to_apply=%region_9.11 | all-reduce | flops 128 | bytes 1024 | tf_op jit(solution)/shard_map/psum | solution.py:48
  945.2 0.7 multiply_convert_fusion
  946.0 33.5 %all-gather.8.cloned.1.call-done = bf16[4096,128]{0,1:T(8,128)(2,1)} async-done(((bf16[256,128]{0,1:T(8,128)(2,1)}), bf16[4096,128]{0,1:T(8,128)(2,1)}) %all-gather.8.cloned.1.call-update) | async-done | bytes 1048592 | tf_op jit(solution)/shard_map/all_gather | solution.py:28
  979.5 2.3 copy.31
  981.8 1.5 reshape.55
  983.3 3.2 gather_fusion.2
  986.5 1.9 fusion.12
  988.4 0.6 copy.44
  989.0 3.6 convolution_bitcast_fusion
  992.6 5.6 copy.33
  998.2 10.6 scatter_custom_fusion.2
  1008.8 1.7 convert_element_type.45
  1010.5 1.3 convert_element_type.46
  1011.8 2.3 copy.34
  1014.1 0.3 fusion.45
  1014.4 0.4 fusion.43
  1014.8 0.5 convolution_add_fusion.3
  1015.3 0.9 convolution_add_fusion.2
  1016.2 74.7 %reduce-scatter.8.cloned.1.call-done = bf16[256,128]{0,1:T(8,128)(2,1)} async-done(((bf16[4096,128]{0,1:T(8,128)(2,1)}), bf16[256,128]{0,1:T(8,128)(2,1)}) %reduce-scatter.8.cloned.1.call-update) | async-done | bytes 65552 | tf_op jit(solution)/shard_map/reduce_scatter | solution.py:35
  1090.9 1.3 convolution_add_fusion.1
  1092.2 0.9 convolution_add_fusion
  (47 shorter events, 1.3 us)
Async XLA Ops:
  7.2 53.3 %copy-start = (bf16[1,1,64,128,128]{4,3,2,1,0:T(8,128)(2,1)S(1)}, bf16[1,1,64,128,128]{4,3,2,1,0:T(8,128)(2,1)}, u32[]{:S(2)}) copy-start(bf16[1,1,64,128,128]{4,3,2,1,0:T(8,128)(2,1)} %param.12) | copy-start | bytes 6291460
  7.2 43.8 %all-gather.4.cloned.1.call-start = ((), (), s32[]{:S(2)}) async-start(), calls=%async_computation.3 | async-start | bytes 1114112 | tf_op jit(solution)/shard_map/all_gather | solution.py:28
  9.7 152.7 %reduce-scatter.4.cloned.1.call-start = ((), (), s32[]{:S(2)}) async-start(), calls=%async_computation.4 | async-start | bytes 1114112 | tf_op jit(solution)/shard_map/reduce_scatter | solution.py:35
  83.3 79.2 %copy-start.1 = (f32[256,128]{1,0:T(8,128)S(1)}, f32[256,128]{1,0:T(8,128)}, u32[]{:S(2)}) copy-start(f32[256,128]{1,0:T(8,128)} %param.10) | copy-start | bytes 393220
  83.3 79.2 %copy-start.11 = (f32[256]{0:T(256)S(1)}, f32[256]{0:T(256)}, u32[]{:S(2)}) copy-start(f32[256]{0:T(256)} %param.11) | copy-start | bytes 3076
  85.6 320.6 %all-reduce.3.cloned.1.call-start = ((), (), s32[]{:S(2)}) async-start(), calls=%async_computation.5 | async-start | bytes 131072 | tf_op jit(solution)/shard_map/psum | solution.py:46
  164.2 352.2 %all-gather.6.cloned.1.call-start = ((), (), s32[]{:S(2)}) async-start(), calls=%async_computation.6 | async-start | bytes 1114112 | tf_op jit(solution)/shard_map/all_gather | solution.py:28
  481.6 0.5 copy-start.12
  482.9 145.0 %reduce-scatter.6.cloned.1.call-start = ((), (), s32[]{:S(2)}) async-start(), calls=%async_computation.7 | async-start | bytes 1114112 | tf_op jit(solution)/shard_map/reduce_scatter | solution.py:35
  548.7 2.6 copy-start.10
  548.7 2.6 copy-start.13
  548.7 81.2 %copy-start.9 = (bf16[256,128]{0,1:T(8,128)(2,1)S(1)}, bf16[256,128]{0,1:T(8,128)(2,1)}, u32[]{:S(2)}) copy-start(bf16[256,128]{0,1:T(8,128)(2,1)} %reduce-scatter.4.cloned.1.call-done) | copy-start | bytes 196612
  551.0 318.8 %all-reduce.5.cloned.1.call-start = ((), (), s32[]{:S(2)}) async-start(), calls=%async_computation.8 | async-start | bytes 131072 | tf_op jit(solution)/shard_map/psum | solution.py:46
  551.8 427.7 %copy-start.4 = (f32[256,128]{1,0:T(8,128)}, f32[256,128]{1,0:T(8,128)S(1)}, u32[]{:S(2)}) copy-start(f32[256,128]{1,0:T(8,128)S(1)} %fusion.29) | copy-start | bytes 393220
  552.1 427.4 %copy-start.2 = (f32[256,128]{1,0:T(8,128)}, f32[256,128]{1,0:T(8,128)S(1)}, u32[]{:S(2)}) copy-start(f32[256,128]{1,0:T(8,128)S(1)} %convolution_add_fusion.5) | copy-start | bytes 393220
  629.2 0.6 copy-start.6
  631.2 348.3 %all-gather.8.cloned.1.call-start = ((), (), s32[]{:S(2)}) async-start(), calls=%async_computation.9 | async-start | bytes 1114112 | tf_op jit(solution)/shard_map/all_gather | solution.py:28
  945.9 145.0 %reduce-scatter.8.cloned.1.call-start = ((), (), s32[]{:S(2)}) async-start(), calls=%async_computation.10 | async-start | bytes 1114112 | tf_op jit(solution)/shard_map/reduce_scatter | solution.py:35
  1011.8 2.3 copy-start.3
  1011.8 2.4 copy-start.8
  1011.8 3.5 copy-start.5
  1014.1 78.1 %copy-start.7 = (f32[256,128]{1,0:T(8,128)S(1)}, f32[256,128]{1,0:T(8,128)}, u32[]{:S(2)}) copy-start(f32[256,128]{1,0:T(8,128)} %copy-done.6) | copy-start | bytes 393220
Sparse Core Ops, SparseCore 0:
  10.3 40.5 all-gather.3
  85.7 76.6 reduce-scatter.3
  169.4 236.6 all-reduce.2
  483.0 33.3 all-gather.5
  551.2 76.6 reduce-scatter.5
  633.3 236.4 all-reduce.4
  946.1 33.3 all-gather.7
  1014.2 76.6 reduce-scatter.7
where the time goes:
time: 1110 us; the launch traced here: 1100 us
  waiting for transfers between devices  814 us (73%)
  blocking collectives  148 us (13%)
  local copies, waits for them, and re-layouts  52.7 us (5%)
  other arithmetic  46.7 us (4%)
  matrix products  22.4 us (2%)
  between operations  15.4 us (1%)
    psum x2, waiting for transfers between devices, residual_block(): gram = lax.psum(inner(block, image), ('row', 'col')) / verts_all  480 us
    reduce_scatter x3, waiting for transfers between devices, apply_operator(): lax.psum_scatter(partial_value.astype(jnp.bfloat16), 'row', scatter_dimen...  227 us
    psum x2, blocking collectives, residual_block(): colsq = lax.psum(jnp.sum(resid * resid, axis=0), ('row', 'col'))  148 us
    all_gather x3, waiting for transfers between devices, apply_operator(): gathered = lax.all_gather(scaled, 'col', axis=0, tiled=True)  106 us
    scatter-add x3, other arithmetic, place_rows(): placed = jax.ops.segment_sum(tile_out, rows_slot, num_segments=row_tiles)  31.9 us
  transfers between devices with their start and end apart: 8, of which 8 were waited for; matrix products, arithmetic and copies ran while one was open for 0% of the time, Pallas kernels for 0%

commit v1 on v0

--- a/solution.py
+++ b/solution.py
@@ -25,7 +25,22 @@
     width_k = block.shape[1]
     slot_total = tiles_here.shape[0]
     scaled = (vertex_scale[:, None] * block).astype(jnp.bfloat16)
-    gathered = lax.all_gather(scaled, "col", axis=0, tiled=True)
+    size, mine, rows = (lax.axis_size("col"), lax.axis_index("col"), scaled.shape[0])
+    forward = [(i, (i + 1) % size) for i in range(size)]
+    backward = [(i, (i - 1) % size) for i in range(size)]
+    out = jnp.zeros((*scaled.shape[:0], size * rows, *scaled.shape[0 + 1 :]), scaled.dtype)
+    out = lax.dynamic_update_slice_in_dim(out, scaled, mine * rows, axis=0)
+    from_left = from_right = scaled
+    halfway = size // 2
+    for step in range(1, halfway + 1):
+        from_left = lax.ppermute(from_left, "col", forward)
+        out = lax.dynamic_update_slice_in_dim(out, from_left, (mine - step) % size * rows, axis=0)
+        if step < size - halfway:
+            from_right = lax.ppermute(from_right, "col", backward)
+            out = lax.dynamic_update_slice_in_dim(
+                out, from_right, (mine + step) % size * rows, axis=0
+            )
+    gathered = out
     flat_panel = gathered.reshape(gathered.shape[0] // tile_side, tile_side * width_k)
     row_tiles = lax.axis_size("row") * block.shape[0] // tile_side
     tile_out = tile_products(

time: 1110 us -> 1120 us (level)
  waiting for transfers between devices: 814 us -> 724 us
  starting transfers between devices: 0.72 us -> 65.1 us
  local copies, waits for them, and re-layouts: 52.7 us -> 85.1 us
    all_gather x3 -> x0, waiting for transfers between devices: 106 us -> none  [apply_operator(): gathered = lax.all_gather(scaled, 'col', axis=0, tiled=True)]
    ppermute x0 -> x45, starting transfers between devices: none -> 64.7 us  [the longest x21 64.3 us: apply_operator(): from_right = lax.ppermute(from_right, 'col', backward)]
    dynamic_update_slice x0 -> x48, local copies, waits for them, and re-layouts: none -> 30 us  [the longest x24 15.1 us: apply_operator(): lax.dynamic_update_slice_in_dim(out, from_left, (mine - step) % size * ro...]
    ppermute x0 -> x45, waiting for transfers between devices: none -> 21.1 us  [the longest x24 21.1 us: apply_operator(): from_left = lax.ppermute(from_left, 'col', forward)]
  transfers between devices with their start and end apart: 8 -> 50, of which waited for: 8 -> 28; matrix products, arithmetic and copies ran while one was open for 0% -> 4% of each run, Pallas kernels for 0% -> 0%
where the time goes in v1:
time: 1120 us; the launch traced here: 1110 us
  waiting for transfers between devices  724 us (65%)
  blocking collectives  149 us (13%)
  local copies, waits for them, and re-layouts  85.1 us (8%)
  starting transfers between devices  65.1 us (6%)
  other arithmetic  45.5 us (4%)
  matrix products  22.5 us (2%)
  between operations  16 us (1%)
    psum x2, waiting for transfers between devices, residual_block(): gram = lax.psum(inner(block, image), ('row', 'col')) / verts_all  480 us
    reduce_scatter x3, waiting for transfers between devices, apply_operator(): lax.psum_scatter(partial_value.astype(jnp.bfloat16), 'row', scatter_dimen...  222 us
    psum x2, blocking collectives, residual_block(): colsq = lax.psum(jnp.sum(resid * resid, axis=0), ('row', 'col'))  149 us
    ppermute x21, starting transfers between devices, apply_operator(): from_right = lax.ppermute(from_right, 'col', backward)  64.3 us
    scatter-add x3, other arithmetic, place_rows(): placed = jax.ops.segment_sum(tile_out, rows_slot, num_segments=row_tiles)  32.6 us
  transfers between devices with their start and end apart: 50, of which 28 were waited for; matrix products, arithmetic and copies ran while one was open for 4% of the time, Pallas kernels for 0%

profile of v1, /device:TPU:2, one launch (start us, length us, event | category | flops | bytes accessed | tf_op | source)
XLA Modules:
  0.0 1106.8 jit_solution(3525400662346640316)
XLA Ops:
  7.2 1.1 copy.86
  9.1 5.3 collective-permute-start.1
  19.4 3.0 collective-permute-start.3
  24.4 2.9 collective-permute-start.5
  29.4 3.0 collective-permute-start.7
  34.5 3.0 collective-permute-start.9
  39.5 2.9 collective-permute-start.11
  44.5 3.0 collective-permute-start.13
  50.2 3.5 collective-permute-done.14
  54.4 1.5 reshape.49
  56.0 3.2 gather_fusion
  59.2 1.9 fusion.14
  61.7 3.6 convolution_bitcast_fusion.2
  65.3 5.6 copy.84
  70.9 10.7 scatter_custom_fusion
  81.6 1.7 convert_element_type.37
  83.3 1.3 convert_element_type.38
  84.6 2.3 copy.85
  87.0 78.2 %reduce-scatter.4.cloned.1.call-done = bf16[256,128]{0,1:T(8,128)(2,1)} async-done(((bf16[4096,128]{0,1:T(8,128)(2,1)}), bf16[256,128]{0,1:T(8,128)(2,1)}) %reduce-scatter.4.cloned.1.call-update) | async-done | bytes 65552 | tf_op jit(solution)/shard_map/reduce_scatter | solution.py:50
  165.2 1.7 convolution_bitcast_fusion.4
  167.2 241.6 %all-reduce.3.cloned.1.call-done = f32[128,128]{0,1:T(8,128)} async-done(((f32[128,128]{0,1:T(8,128)}), f32[128,128]{0,1:T(8,128)}) %all-reduce.3.cloned.1.call-update) | async-done | bytes 65552 | tf_op jit(solution)/shard_map/psum | solution.py:61
  408.8 1.2 multiply_reduce_fusion.1
  410.0 74.2 %psum.29 = f32[128]{0:T(128)S(1)} all-reduce(f32[128]{0:T(128)S(1)} %get-tuple-element.3), channel_id=1, replica_groups=mesh['row'=16,'col'=16] {'row','col'}, use_global_device_ids=true, to_apply=%region_4.6 | all-reduce | flops 128 | bytes 1024 | tf_op jit(solution)/shard_map/psum | solution.py:63
  485.0 2.9 collective-permute-start.16
  490.8 3.0 collective-permute-start.18
  495.8 2.9 collective-permute-start.20
  500.8 3.0 collective-permute-start.22
  505.9 3.0 collective-permute-start.24
  510.9 2.9 collective-permute-start.26
  515.9 3.0 collective-permute-start.28
  521.6 3.5 collective-permute-done.29
  525.8 1.5 reshape.52
  527.4 3.2 gather_fusion.1
  530.6 1.9 fusion.13
  533.1 3.6 convolution_bitcast_fusion.1
  536.7 5.6 copy.104
  542.3 10.9 scatter_custom_fusion.1
  553.2 1.7 convert_element_type.41
  554.9 1.3 convert_element_type.42
  556.2 2.3 copy.105
  559.4 72.7 %reduce-scatter.6.cloned.1.call-done = bf16[256,128]{0,1:T(8,128)(2,1)} async-done(((bf16[4096,128]{0,1:T(8,128)(2,1)}), bf16[256,128]{0,1:T(8,128)(2,1)}) %reduce-scatter.6.cloned.1.call-update) | async-done | bytes 65552 | tf_op jit(solution)/shard_map/reduce_scatter | solution.py:50
  632.1 1.3 fusion.22
  635.4 238.7 %all-reduce.5.cloned.1.call-done = f32[128,128]{0,1:T(8,128)} async-done(((f32[128,128]{0,1:T(8,128)}), f32[128,128]{0,1:T(8,128)}) %all-reduce.5.cloned.1.call-update) | async-done | bytes 65552 | tf_op jit(solution)/shard_map/psum | solution.py:61
  874.2 1.2 multiply_reduce_fusion
  875.4 74.5 %psum.31 = f32[128]{0:T(128)S(1)} all-reduce(f32[128]{0:T(128)S(1)} %get-tuple-element.5), channel_id=1, replica_groups=mesh['row'=16,'col'=16] {'row','col'}, use_global_device_ids=true, to_apply=%region_9.11 | all-reduce | flops 128 | bytes 1024 | tf_op jit(solution)/shard_map/psum | solution.py:63
  950.3 3.0 collective-permute-start.31
  956.1 3.0 collective-permute-start.33
  961.2 2.9 collective-permute-start.35
  966.2 2.9 collective-permute-start.37
  971.2 3.0 collective-permute-start.39
  976.3 2.9 collective-permute-start.41
  981.3 2.9 collective-permute-start.43
  987.0 3.5 collective-permute-done.44
  991.2 1.5 reshape.55
  992.7 3.2 gather_fusion.2
  996.0 1.9 fusion.12
  998.4 3.6 convolution_bitcast_fusion
  1002.1 5.6 copy.126
  1007.7 11.0 scatter_custom_fusion.2
  1018.7 1.7 convert_element_type.45
  1020.4 1.3 convert_element_type.46
  1021.7 2.3 copy.127
  1026.1 71.4 %reduce-scatter.8.cloned.1.call-done = bf16[256,128]{0,1:T(8,128)(2,1)} async-done(((bf16[4096,128]{0,1:T(8,128)(2,1)}), bf16[256,128]{0,1:T(8,128)(2,1)}) %reduce-scatter.8.cloned.1.call-update) | async-done | bytes 65552 | tf_op jit(solution)/shard_map/reduce_scatter | solution.py:50
  1097.5 1.3 convolution_add_fusion.1
  (228 shorter events, 60.6 us)
Async XLA Ops:
  7.2 54.5 %copy-start = (bf16[1,1,64,128,128]{4,3,2,1,0:T(8,128)(2,1)S(1)}, bf16[1,1,64,128,128]{4,3,2,1,0:T(8,128)(2,1)}, u32[]{:S(2)}) copy-start(bf16[1,1,64,128,128]{4,3,2,1,0:T(8,128)(2,1)} %param.12) | copy-start | bytes 6291460
  7.2 158.1 %reduce-scatter.4.cloned.1.call-start = ((), (), s32[]{:S(2)}) async-start(), calls=%async_computation.3 | async-start | bytes 1114112 | tf_op jit(solution)/shard_map/reduce_scatter | solution.py:50
  9.1 9.4 collective-permute-start
  9.1 10.2 collective-permute-start.1
  18.6 4.9 collective-permute-start.2
  19.4 4.9 collective-permute-start.3
  23.6 4.9 collective-permute-start.4
  24.4 4.9 collective-permute-start.5
  28.7 4.9 collective-permute-start.6
  29.4 4.9 collective-permute-start.7
  33.7 4.9 collective-permute-start.8
  34.5 4.9 collective-permute-start.9
  38.7 4.9 collective-permute-start.10
  39.5 4.9 collective-permute-start.11
  43.8 4.9 collective-permute-start.12
  44.5 4.9 collective-permute-start.13
  48.8 4.9 collective-permute-start.14
  84.6 80.6 %copy-start.1 = (f32[256,128]{1,0:T(8,128)S(1)}, f32[256,128]{1,0:T(8,128)}, u32[]{:S(2)}) copy-start(f32[256,128]{1,0:T(8,128)} %param.10) | copy-start | bytes 393220
  84.6 80.6 %copy-start.11 = (f32[256]{0:T(256)S(1)}, f32[256]{0:T(256)}, u32[]{:S(2)}) copy-start(f32[256]{0:T(256)} %param.11) | copy-start | bytes 3076
  87.0 321.8 %all-reduce.3.cloned.1.call-start = ((), (), s32[]{:S(2)}) async-start(), calls=%async_computation.4 | async-start | bytes 131072 | tf_op jit(solution)/shard_map/psum | solution.py:61
  167.0 465.1 %reduce-scatter.6.cloned.1.call-start = ((), (), s32[]{:S(2)}) async-start(), calls=%async_computation.5 | async-start | bytes 1114112 | tf_op jit(solution)/shard_map/reduce_scatter | solution.py:50
  485.0 4.9 collective-permute-start.15
  485.0 5.7 collective-permute-start.16
  490.0 4.9 collective-permute-start.17
  490.8 4.9 collective-permute-start.18
  495.0 4.9 collective-permute-start.19
  495.8 4.9 collective-permute-start.20
  500.1 4.9 collective-permute-start.21
  500.8 4.9 collective-permute-start.22
  505.1 4.9 collective-permute-start.23
  505.9 4.9 collective-permute-start.24
  510.1 4.9 collective-permute-start.25
  510.9 4.9 collective-permute-start.26
  515.2 4.9 collective-permute-start.27
  515.9 4.9 collective-permute-start.28
  520.2 4.9 collective-permute-start.29
  556.2 2.4 copy-start.10
  556.2 2.4 copy-start.13
  556.2 77.9 %copy-start.9 = (bf16[256,128]{0,1:T(8,128)(2,1)S(1)}, bf16[256,128]{0,1:T(8,128)(2,1)}, u32[]{:S(2)}) copy-start(bf16[256,128]{0,1:T(8,128)(2,1)} %reduce-scatter.4.cloned.1.call-done) | copy-start | bytes 196612
  558.6 315.6 %all-reduce.5.cloned.1.call-start = ((), (), s32[]{:S(2)}) async-start(), calls=%async_computation.6 | async-start | bytes 131072 | tf_op jit(solution)/shard_map/psum | solution.py:61
  559.1 396.9 %copy-start.4 = (f32[256,128]{1,0:T(8,128)}, f32[256,128]{1,0:T(8,128)S(1)}, u32[]{:S(2)}) copy-start(f32[256,128]{1,0:T(8,128)S(1)} %fusion.29) | copy-start | bytes 393220
  559.4 401.0 %copy-start.2 = (f32[256,128]{1,0:T(8,128)}, f32[256,128]{1,0:T(8,128)S(1)}, u32[]{:S(2)}) copy-start(f32[256,128]{1,0:T(8,128)S(1)} %convolution_add_fusion.5) | copy-start | bytes 393220
  633.4 0.7 copy-start.6
  635.4 462.1 %reduce-scatter.8.cloned.1.call-start = ((), (), s32[]{:S(2)}) async-start(), calls=%async_computation.7 | async-start | bytes 1114112 | tf_op jit(solution)/shard_map/reduce_scatter | solution.py:50
  950.3 4.9 collective-permute-start.30
  950.3 5.7 collective-permute-start.31
  955.4 4.9 collective-permute-start.32
  956.1 4.9 collective-permute-start.33
  960.4 4.9 collective-permute-start.34
  961.2 4.9 collective-permute-start.35
  965.4 4.9 collective-permute-start.36
  966.2 4.9 collective-permute-start.37
  970.5 4.9 collective-permute-start.38
  971.2 4.9 collective-permute-start.39
  975.5 4.9 collective-permute-start.40
  976.3 4.9 collective-permute-start.41
  980.5 4.9 collective-permute-start.42
  981.3 4.9 collective-permute-start.43
  985.6 4.9 collective-permute-start.44
  1021.7 2.4 copy-start.3
  1021.7 2.4 copy-start.8
  1021.7 3.1 copy-start.15
  1021.7 3.5 copy-start.5
  1024.0 74.8 %copy-start.7 = (f32[256,128]{1,0:T(8,128)S(1)}, f32[256,128]{1,0:T(8,128)}, u32[]{:S(2)}) copy-start(f32[256,128]{1,0:T(8,128)} %copy-done.6) | copy-start | bytes 393220
  (2 other events, 1.0 us)
Sparse Core Ops, SparseCore 0:
  87.1 78.0 reduce-scatter.3
  172.2 236.5 all-reduce.2
  558.7 73.3 reduce-scatter.5
  637.4 236.6 all-reduce.4
  1024.2 73.2 reduce-scatter.7
